TPU v7x, 512 devices: a whole 4x4x16 slice. The times are simulated.
512 devices in a mesh: chol: 8 (over x, y_hi), walk: 64 (over z, y_lo, core).
Axes of the slice: x: 4, y: 4 (y_hi: 2, y_lo: 2; y = y_hi * 2 + y_lo), z: 16, core: 2. Of those that a mesh axis runs over, the one named last changes fastest.
Arguments:
- field_draws: bfloat16 [64, 2048], P('walk', 'chol'), may hold values from -6 to 6
- chol_vectors: bfloat16 [2048, 512, 512], P('chol', 'walk'), as said below
- rotated_vectors: bfloat16 [2048, 128, 512], P(('chol', 'walk')), may hold values from -1.5 to 1.5
- walkers: bfloat16 [64, 512, 128], P('walk'), may hold values from -6 to 6
Outputs:
- propagated: float32 [64, 512, 128], P('walk')
- exchange_energy: float32 [64], P('walk')
Inputs may be any that keep to these rules, and one draw needn't show every extreme that they name: Each chol_vectors[g] is a symmetric matrix.
All inputs are finite; a program needn't handle non-finite values.
Results may differ from a plain program's by a relative error of at most 0.0036.
Values may be sent and summed in bfloat16 or wider, within the bound.
A program may use at most 64 MiB of HBM per device.

v0:
```python
import jax
import jax.numpy as jnp
from jax import lax
from jax.sharding import PartitionSpec as P

OCC = 128
TERMS = 4


def solve_dual(correlation, transposed):
    gram = jnp.dot(correlation, correlation.T, precision=lax.Precision.HIGHEST)
    factor = jnp.linalg.cholesky(gram)
    right = jnp.dot(correlation, transposed, precision=lax.Precision.HIGHEST)
    return jax.scipy.linalg.cho_solve((factor, True), right)


def energy_folder(rotated_vectors):

    def accumulate(totals, columns, offset):
        walker_count = columns.shape[1] // OCC

        def vector_step(vector, summed):
            single = lax.dynamic_index_in_dim(rotated_vectors, vector, 0, keepdims=False)
            products = jnp.dot(single, columns, preferred_element_type=jnp.float32)
            tiled = products.reshape(OCC, walker_count, OCC)
            return summed + jnp.einsum("iwj,jwi->w", tiled, tiled)

        contrib = lax.fori_loop(
            0, rotated_vectors.shape[0], vector_step, jnp.zeros((walker_count,), jnp.float32)
        )
        return contrib

    return accumulate


def per_device(field_draws, chol_vectors, rotated_vectors, walkers):
    local_walkers = walkers.shape[0]
    walk_count = lax.axis_size("walk")
    total_walkers = local_walkers * walk_count
    slab_vectors, slab_rows, orbitals = chol_vectors.shape
    all_draws = lax.all_gather(field_draws, "walk", axis=0, tiled=True)
    partial_rows = jnp.dot(
        all_draws,
        chol_vectors.reshape(slab_vectors, slab_rows * orbitals),
        preferred_element_type=jnp.float32,
    )
    partial_rows = partial_rows.reshape(total_walkers, slab_rows, orbitals)
    gathered = lax.all_to_all(partial_rows, "walk", split_axis=0, concat_axis=1, tiled=True)
    operators = lax.psum(gathered, "chol").astype(jnp.bfloat16)
    taylor_term = walkers
    propagated = walkers.astype(jnp.float32)
    for degree in range(1, TERMS + 1):
        applied = jnp.einsum(
            "wpq,wqi->wpi", operators, taylor_term, preferred_element_type=jnp.float32
        )
        taylor_term = (applied / degree).astype(jnp.bfloat16)
        propagated = propagated + taylor_term.astype(jnp.float32)
    correlation = jnp.einsum(
        "wpi,wpj->wij", walkers.astype(jnp.float32), propagated, precision=lax.Precision.HIGHEST
    )
    dual_t = jax.vmap(solve_dual)(correlation, jnp.transpose(propagated, (0, 2, 1)))
    dual_cols = (
        jnp.transpose(dual_t, (2, 0, 1)).reshape(orbitals, local_walkers * OCC).astype(jnp.bfloat16)
    )
    accumulate = energy_folder(rotated_vectors)
    empty = jnp.zeros((total_walkers,), jnp.float32)
    totals = accumulate(empty, lax.all_gather(dual_cols, "walk", axis=1, tiled=True), jnp.int32(0))
    summed = lax.psum(totals, ("chol", "walk"))
    mine = lax.dynamic_slice_in_dim(
        summed, lax.axis_index("walk") * local_walkers, local_walkers, 0
    )
    return (propagated, -0.5 * mine)


def solution(mesh):
    return jax.shard_map(
        per_device,
        mesh=mesh,
        in_specs=(
            P("walk", "chol"),
            P("chol", "walk", None),
            P(("chol", "walk"), None, None),
            P("walk", None, None),
        ),
        out_specs=(P("walk", None, None), P("walk")),
        check_vma=False,
    )
```

profile of v0, /device:TPU:1, one launch (start us, length us, event | category | flops | bytes accessed | tf_op | source)
XLA Modules:
  0.0 557.0 jit_solution(8198773161770312766)
XLA Ops:
  7.2 3.8 copy.31
  11.1 3.3 copy.19
  14.3 71.2 %all-gather.1 = bf16[64,1,256]{2,1,0:T(2,128)(2,1)S(1)} all-gather(bf16[1,1,256]{2,1,0:T(2,128)(2,1)S(1)} %bitcast.101), channel_id=1, replica_groups=mesh['chol'=8,'walk'=64] {'walk'}, dimensions={0}, use_global_device_ids=true | all-gather | bytes 33280 | tf_op jit(solution)/shard_map/all_gather | solution.py:41
  85.6 0.7 fusion.27
  87.0 60.6 %all_to_all.12 = f32[64,8,512]{2,1,0:T(8,128)S(1)} all-to-all(f32[64,8,512]{2,1,0:T(8,128)S(1)} %copy.20), channel_id=1, replica_groups=mesh['chol'=8,'walk'=64] {'walk'}, dimensions={0} | all-to-all | bytes 2097152 | tf_op jit(solution)/shard_map/all_to_all | solution.py:48
  147.5 68.4 %all-reduce.1 = bf16[1,512,512]{2,1,0:T(8,128)(2,1)S(1)} all-reduce(f32[1,512,512]{2,1,0:T(8,128)S(1)} %bitcast.98), channel_id=1, replica_groups=mesh['chol'=8,'walk'=64] {'chol'}, use_global_device_ids=true, to_apply=%region_0.0 | all-reduce | flops 262144 | bytes 1572864 | tf_op jit(solution)/shard_map/psum | solution.py:49
  218.4 11.7 %custom-call.11 = f32[1,128,128]{2,1,0:T(8,128)S(1)} custom-call(f32[1,128,128]{2,1,0:T(8,128)S(1)} %fusion.23), custom_call_target="Cholesky" | custom-call | tf_op jit(solution)/shard_map/vmap(jit(cholesky))/cholesky | solution.py:12
  231.5 9.8 %custom-call.12 = f32[1,1,128,128]{2,3,1,0:T(8,128)S(1)} custom-call(f32[1,1,128,128]{3,2,1,0:T(8,128)S(1)} %fusion.22), custom_call_target="InvertDiagBlocksLowerTriangular" | custom-call | tf_op jit(solution)/shard_map/vmap(jit(_cho_solve))/triangular_solve | solution.py:14
  241.7 1.0 fusion.11
  242.8 131.1 %all-gather.4.cloned.1.call-done = bf16[512,1,8192]{0,2,1:T(8,128)(2,1)} async-done(((bf16[512,1,128]{0,2,1:T(8,128)(2,1)}), bf16[512,1,8192]{0,2,1:T(8,128)(2,1)}) %all-gather.4.cloned.1.call-update) | async-done | bytes 8388624 | tf_op jit(solution)/shard_map/all_gather | solution.py:67
  373.9 71.8 %while.14 = (s32[]{:T(128)}, f32[64]{0:T(128)S(1)}, bf16[4,128,512]{2,1,0:T(8,128)(2,1)}, bf16[512,8192]{0,1:T(8,128)(2,1)}, s32[]{:T(128)}, /*index=5*/s32[]{:T(128)}) while((s32[]{:T(128)}, f32[64]{0:T(128)S(1)}, bf16[4,128,512]{2,1,0:T(8,128)(2,1)}, bf16[512,8192]{0,1:T(8,128)(2,1)}, s32[]{:T(128)}, /*index=5*/s32[]{:T(128)}) %tuple.43), condition=%wide.region_4.5_spmd.clone, body=%wide.region_3.4_spmd.clone.sunk | while | flops 1075839104 | bytes 29492812 | solution.py:28
  373.9 8.2 %fusion.47 = f32[128,64,128]{2,0,1:T(8,128)} fusion(bf16[64,128,512]{2,1,0:T(8,128)(2,1)} %bitcast.95, bf16[4,128,512]{2,1,0:T(8,128)(2,1)} %get-tuple-element.152, s32[]{:T(128)} %get-tuple-element.144), kind=kOutput, calls=%fused_computation.1.clone.1 | convolution fusion | flops 1073741824 | bytes 12714496 | tf_op jit(solution)/shard_map/while/body/eval_jaxpr/dot_general | solution.py:24
  382.1 5.6 %copy.37 = f32[64,128,128]{1,2,0:T(8,128)} copy(f32[64,128,128]{2,1,0:T(8,128)} %bitcast.93) | data formatting | bytes 8388608 | tf_op jit(solution)/shard_map/while
  387.7 4.0 multiply_reduce_fusion.2
  391.8 8.3 %fusion.47 = f32[128,64,128]{2,0,1:T(8,128)} fusion(bf16[64,128,512]{2,1,0:T(8,128)(2,1)} %bitcast.95, bf16[4,128,512]{2,1,0:T(8,128)(2,1)} %get-tuple-element.152, s32[]{:T(128)} %get-tuple-element.144), kind=kOutput, calls=%fused_computation.1.clone.1 | convolution fusion | flops 1073741824 | bytes 12714496 | tf_op jit(solution)/shard_map/while/body/eval_jaxpr/dot_general | solution.py:24
  400.1 5.6 %copy.37 = f32[64,128,128]{1,2,0:T(8,128)} copy(f32[64,128,128]{2,1,0:T(8,128)} %bitcast.93) | data formatting | bytes 8388608 | tf_op jit(solution)/shard_map/while
  405.7 4.0 multiply_reduce_fusion.2
  409.7 8.3 %fusion.47 = f32[128,64,128]{2,0,1:T(8,128)} fusion(bf16[64,128,512]{2,1,0:T(8,128)(2,1)} %bitcast.95, bf16[4,128,512]{2,1,0:T(8,128)(2,1)} %get-tuple-element.152, s32[]{:T(128)} %get-tuple-element.144), kind=kOutput, calls=%fused_computation.1.clone.1 | convolution fusion | flops 1073741824 | bytes 12714496 | tf_op jit(solution)/shard_map/while/body/eval_jaxpr/dot_general | solution.py:24
  418.0 5.6 %copy.37 = f32[64,128,128]{1,2,0:T(8,128)} copy(f32[64,128,128]{2,1,0:T(8,128)} %bitcast.93) | data formatting | bytes 8388608 | tf_op jit(solution)/shard_map/while
  423.6 4.0 multiply_reduce_fusion.2
  427.7 8.3 %fusion.47 = f32[128,64,128]{2,0,1:T(8,128)} fusion(bf16[64,128,512]{2,1,0:T(8,128)(2,1)} %bitcast.95, bf16[4,128,512]{2,1,0:T(8,128)(2,1)} %get-tuple-element.152, s32[]{:T(128)} %get-tuple-element.144), kind=kOutput, calls=%fused_computation.1.clone.1 | convolution fusion | flops 1073741824 | bytes 12714496 | tf_op jit(solution)/shard_map/while/body/eval_jaxpr/dot_general | solution.py:24
  435.9 5.6 %copy.37 = f32[64,128,128]{1,2,0:T(8,128)} copy(f32[64,128,128]{2,1,0:T(8,128)} %bitcast.93) | data formatting | bytes 8388608 | tf_op jit(solution)/shard_map/while
  441.6 4.0 multiply_reduce_fusion.2
  445.6 102.2 %psum.15 = f32[64]{0:T(128)S(1)} all-reduce(f32[64]{0:T(128)S(1)} %get-tuple-element.81), channel_id=1, replica_groups=mesh['chol'=8,'walk'=64] {'chol','walk'}, use_global_device_ids=true, to_apply=%region_5.6 | all-reduce | flops 64 | bytes 512 | tf_op jit(solution)/shard_map/psum | solution.py:68
  (28 shorter events, 5.4 us)
Async XLA Ops:
  7.2 366.7 %all-gather.4.cloned.1.call-start = ((), (), s32[]{:S(2)}) async-start(), calls=%async_computation.1 | async-start | bytes 8519680 | tf_op jit(solution)/shard_map/all_gather | solution.py:67
  7.2 7.1 %copy-start.2 = (bf16[1,256]{1,0:T(2,128)(2,1)S(1)}, bf16[1,256]{1,0:T(2,128)(2,1)}, u32[]{:S(2)}) copy-start(bf16[1,256]{1,0:T(2,128)(2,1)} %param.6) | copy-start | bytes 1540
  85.6 130.4 %copy-start.1 = (bf16[1,512,128]{2,1,0:T(8,128)(2,1)S(1)}, bf16[1,512,128]{2,1,0:T(8,128)(2,1)}, u32[]{:S(2)}) copy-start(bf16[1,512,128]{2,1,0:T(8,128)(2,1)} %param.9) | copy-start | bytes 393220
  217.2 156.7 %copy-start = (f32[1,512,128]{2,1,0:T(8,128)}, f32[1,512,128]{2,1,0:T(8,128)S(1)}, u32[]{:S(2)}) copy-start(f32[1,512,128]{2,1,0:T(8,128)S(1)} %fusion.10) | copy-start | bytes 786436
Sparse Core Ops, SparseCore 0:
  242.9 130.9 all-gather.3
where the time goes:
time: 558 us; the launch traced here: 557 us
  blocking collectives  302 us (54%)
  waiting for transfers between devices  131 us (23%)
  other arithmetic  39.1 us (7%)
  matrix products  37.5 us (7%)
  local copies, waits for them, and re-layouts  30.9 us (6%)
  between operations  16 us (3%)
    all_gather x1, waiting for transfers between devices, per_device(): lax.all_gather(dual_cols, 'walk', axis=1, tiled=True)  131 us
    psum x1, blocking collectives, per_device(): summed = lax.psum(totals, ('chol', 'walk'))  102 us
    all_gather x1, blocking collectives, per_device(): all_draws = lax.all_gather(field_draws, 'walk', axis=0, tiled=True)  71.2 us
    psum x1, blocking collectives, per_device(): operators = lax.psum(gathered, 'chol').astype(jnp.bfloat16)  68.4 us
    all_to_all x1, blocking collectives, per_device(): lax.all_to_all(partial_rows, 'walk', split_axis=0, concat_axis=1, tiled=T...  60.6 us
    dot_general x4, matrix products, vector_step(): products = jnp.dot(single, columns, preferred_element_type=jnp.float32)  33 us
    while x4, local copies, waits for them, and re-layouts  22.5 us
    dot_general x4, other arithmetic, vector_step(): return summed + jnp.einsum('iwj,jwi->w', tiled, tiled)  16.1 us
  transfers between devices with their start and end apart: 1, of which 1 were waited for; matrix products, arithmetic and copies ran while one was open for 0% of the time, Pallas kernels for 0%

commit v1 on v0

v1 whole, which is shorter than its diff:
```python
import functools

import jax
import jax.numpy as jnp
from jax import lax
from jax.experimental import pallas as pl
from jax.experimental.pallas import tpu as pltpu
from jax.sharding import PartitionSpec as P

ORB = 512
OCC = 128
TERMS = 4
SLABS = 64
CHOL = 8
MESH = pl.DeviceIdType.MESH
HIGHEST = lax.Precision.HIGHEST
VMEM = pltpu.VMEM
DMA = pltpu.SemaphoreType.DMA


def here():
    chol = lax.axis_index("chol")
    walk = lax.axis_index("walk")
    return chol, walk


def to(chol, walk):
    return {"chol": chol, "walk": walk}


def gather_kernel(
    draws_ref, chol_hbm, rot_hbm, oper_ref, rall_ref,
    chol_buf, gathered, acc, part, recv, red,
    chol_sem, rot_sem, draw_send, draw_recv, part_send, part_recv,
    row_send, row_recv, x_send, x_recv, sib_send, sib_recv,
):
    chol, walk = here()
    z = walk // 4
    core = walk % 2
    x = chol // 2
    y_hi = chol % 2
    sibling = walk + 1 - 2 * core
    barrier = pltpu.get_barrier_semaphore()

    def greet_walk(i, carry):
        pl.semaphore_signal(barrier, inc=1, device_id=to(chol, (walk + i) % 64), device_id_type=MESH)
        return carry

    def greet_chol(i, carry):
        pl.semaphore_signal(barrier, inc=1, device_id=to((chol + i) % 8, walk), device_id_type=MESH)
        return carry

    lax.fori_loop(1, 64, greet_walk, 0)
    lax.fori_loop(1, 8, greet_chol, 0)
    load_chol = pltpu.make_async_copy(chol_hbm, chol_buf, chol_sem)
    load_chol.start()
    load_rot = pltpu.make_async_copy(rot_hbm, rall_ref.at[x, core], rot_sem)
    load_rot.start()
    slot = (z % 8) * 8 + (z // 8) * 4 + walk % 4
    own_draw = pltpu.make_async_copy(draws_ref, gathered.at[slot], draw_recv)
    own_draw.start()
    pl.semaphore_wait(barrier, 70)

    def send_draw(i, carry):
        pltpu.make_async_remote_copy(
            draws_ref, gathered.at[slot], draw_send, draw_recv,
            device_id=to(chol, (walk + i) % 64), device_id_type=MESH,
        ).start()
        return carry

    lax.fori_loop(1, 64, send_draw, 0)

    load_rot.wait()
    mine = rall_ref.at[x, core]

    def x_copy(i):
        peer = ((x + i) % 4) * 2 + y_hi
        return pltpu.make_async_remote_copy(
            mine, mine, x_send.at[i - 1], x_recv.at[i - 1],
            device_id=to(peer, walk), device_id_type=MESH,
        )

    def sib_copy(i):
        block = rall_ref.at[(x + 4 - i) % 4, core]
        return pltpu.make_async_remote_copy(
            block, block, sib_send.at[i], sib_recv.at[i],
            device_id=to(chol, sibling), device_id_type=MESH,
        )

    for i in (1, 2, 3):
        x_copy(i).start()
    sib_copy(0).start()

    load_chol.wait()
    pltpu.make_async_copy(gathered, gathered, draw_recv).wait()

    draws = gathered[...].reshape(SLABS, 256).astype(jnp.bfloat16)
    draws = jnp.broadcast_to(draws.astype(jnp.float32)[:, None, :], (SLABS, 8, 256))
    draws = draws.reshape(SLABS * 8, 256).astype(jnp.bfloat16)
    same_row = (lax.broadcasted_iota(jnp.int32, (512, 256), 0) % 8) == (
        lax.broadcasted_iota(jnp.int32, (512, 256), 1) % 8
    )
    vec_iota = lax.broadcasted_iota(jnp.int32, (256, 256), 0)
    col_iota = lax.broadcasted_iota(jnp.int32, (256, 256), 1) // 8
    acc[...] = jnp.zeros_like(acc)

    def chunk(i, carry):
        pick = jnp.where(vec_iota == col_iota + i * 32, 1.0, 0.0).astype(jnp.bfloat16)
        spread = jnp.dot(draws, pick, preferred_element_type=jnp.float32)
        spread = jnp.where(same_row, spread, 0.0).astype(jnp.bfloat16)
        rows = pl.ds(pl.multiple_of(i * 256, 256), 256)
        acc[...] += jnp.dot(spread, chol_buf[rows, :], preferred_element_type=jnp.float32)
        return carry

    lax.fori_loop(0, 8, chunk, 0)
    for peer in range(CHOL):
        part[peer] = acc[peer * 64 : peer * 64 + 64, :].astype(jnp.bfloat16)

    def part_copy(i):
        peer = (chol + i) % 8
        return pltpu.make_async_remote_copy(
            part.at[peer], recv.at[i - 1], part_send.at[i - 1], part_recv.at[i - 1],
            device_id=to(peer, walk), device_id_type=MESH,
        )

    for i in range(1, 8):
        part_copy(i).start()
    total = part[chol].astype(jnp.float32)
    for i in range(1, 8):
        part_copy(i).wait_recv()
        total = total + recv[i - 1].astype(jnp.float32)
    red[...] = total.astype(jnp.bfloat16).reshape(8, 8, ORB)

    computes = (z % 8) == chol

    def row_target(j):
        return ((j // 4) * 8 + chol) * 4 + j % 4

    def send_rows(j, carry):
        target = row_target(j)

        @pl.when(target != walk)
        def _():
            pltpu.make_async_remote_copy(
                red.at[j], oper_ref.at[walk], row_send.at[j], row_recv,
                device_id=to(chol, target), device_id_type=MESH,
            ).start()

        @pl.when(target == walk)
        def _():
            pltpu.make_async_copy(red.at[j], oper_ref.at[walk], row_recv).start()

        return carry

    lax.fori_loop(0, 8, send_rows, 0)

    for i in (1, 2, 3):
        x_copy(i).wait_recv()
        sib_copy(i).start()

    @pl.when(computes)
    def _():
        pltpu.make_async_copy(oper_ref, oper_ref, row_recv).wait()

    @pl.when(jnp.logical_not(computes))
    def _():
        oper_ref[...] = jnp.zeros_like(oper_ref)

    def drain_rows(j, carry):
        @pl.when(row_target(j) != walk)
        def _():
            pltpu.make_async_remote_copy(
                red.at[j], oper_ref.at[walk], row_send.at[j], row_recv,
                device_id=to(chol, row_target(j)), device_id_type=MESH,
            ).wait_send()

        return carry

    lax.fori_loop(0, 8, drain_rows, 0)
    sent = gathered.at[pl.ds(0, 63)]
    pltpu.make_async_copy(sent, sent, draw_send).wait()
    for i in range(1, 8):
        part_copy(i).wait_send()
    for i in (1, 2, 3):
        x_copy(i).wait_send()
    for i in range(4):
        sib_copy(i).wait()


def gather(draws, chol_vectors, rotated):
    any_ref = pl.BlockSpec(memory_space=pl.ANY)
    vmem = pl.BlockSpec(memory_space=VMEM)
    return pl.pallas_call(
        gather_kernel,
        out_shape=(
            jax.ShapeDtypeStruct((SLABS, 8, ORB), jnp.bfloat16),
            jax.ShapeDtypeStruct((4, 2, 512, ORB), jnp.bfloat16),
        ),
        in_specs=[vmem, any_ref, any_ref],
        out_specs=(vmem, vmem),
        scratch_shapes=[
            VMEM((2048, ORB), jnp.bfloat16),
            VMEM((SLABS, 1, 256), jnp.float32),
            VMEM((512, ORB), jnp.float32),
            VMEM((CHOL, 64, ORB), jnp.bfloat16),
            VMEM((CHOL - 1, 64, ORB), jnp.bfloat16),
            VMEM((8, 8, ORB), jnp.bfloat16),
            DMA, DMA, DMA, DMA, DMA((7,)), DMA((7,)),
            DMA((8,)), DMA, DMA((3,)), DMA((3,)), DMA((4,)), DMA((4,)),
        ],
        compiler_params=pltpu.CompilerParams(collective_id=0, has_side_effects=True),
        name="gather",
    )(draws, chol_vectors, rotated)


def propagate_kernel(oper_ref, walker_ref, prop_ref, dual_ref, corr):
    walker = walker_ref[...]
    term = walker
    total = walker.astype(jnp.float32)
    oper = oper_ref[...]
    for degree in range(1, TERMS + 1):
        applied = jnp.dot(oper, term, preferred_element_type=jnp.float32)
        term = (applied / degree).astype(jnp.bfloat16)
        total = total + term.astype(jnp.float32)
    prop_ref[...] = total
    corr[...] = lax.dot_general(
        walker.astype(jnp.float32), total, (((0,), (0,)), ((), ())), precision=HIGHEST,
        preferred_element_type=jnp.float32,
    )
    lane = lax.broadcasted_iota(jnp.int32, (OCC, OCC), 1)
    sub = lax.broadcasted_iota(jnp.int32, (OCC, OCC), 0)

    def eliminate(k, carry):
        full = corr[...]
        row = corr[pl.ds(k, 1), :]
        here_lane = lane == k
        column = jnp.sum(jnp.where(here_lane, full, 0.0), axis=1, keepdims=True)
        pivot = jnp.sum(jnp.where(here_lane[0:1], row, 0.0), axis=1, keepdims=True)
        inverse = 1.0 / pivot
        scaled = jnp.where(here_lane[0:1], inverse, row * inverse)
        corr[...] = jnp.where(
            sub == k, scaled, jnp.where(here_lane, 0.0, full) - column * scaled
        )
        return carry

    lax.fori_loop(0, OCC, eliminate, 0)
    dual_ref[...] = jnp.dot(
        total, corr[...], precision=HIGHEST, preferred_element_type=jnp.float32
    ).astype(jnp.bfloat16)


def propagate(operator, walker):
    return pl.pallas_call(
        propagate_kernel,
        out_shape=(
            jax.ShapeDtypeStruct((ORB, OCC), jnp.float32),
            jax.ShapeDtypeStruct((ORB, OCC), jnp.bfloat16),
        ),
        scratch_shapes=[VMEM((OCC, OCC), jnp.float32)],
        name="propagate",
    )(operator, walker)


def energy_kernel(
    prop_in, dual_in, rall_hbm, prop_out, energy_out,
    rall, duals, pieces, collected, answer,
    rall_sem, prop_sem, dual_sem, z_send, near_send, z_recv, y_send, y_recv,
    prop_send, prop_recv, piece_send, piece_recv, final_send, final_recv,
):
    chol, walk = here()
    z = walk // 4
    core = walk % 2
    x = chol // 2
    y = (chol % 2) * 2 + (walk // 2) % 2
    computes = (z % 8) == chol
    barrier = pltpu.get_barrier_semaphore()

    def at(zz, yy):
        return to(x * 2 + yy // 2, zz * 4 + (yy % 2) * 2 + core)

    def greet_plane(i, carry):
        spot = (z * 4 + y + i) % 64
        pl.semaphore_signal(barrier, inc=1, device_id=at(spot // 4, spot % 4), device_id_type=MESH)
        return carry

    def greet_chol(i, carry):
        pl.semaphore_signal(barrier, inc=1, device_id=to((chol + i) % 8, walk), device_id_type=MESH)
        return carry

    lax.fori_loop(1, 64, greet_plane, 0)
    lax.fori_loop(1, 8, greet_chol, 0)
    load_rall = pltpu.make_async_copy(rall_hbm, rall, rall_sem)
    load_rall.start()
    half = z // 8
    own = duals.at[y, half]
    hub = (z % 4) == (chol % 4)

    @pl.when(computes)
    def _():
        keep = pltpu.make_async_copy(dual_in, own, dual_sem)
        keep.start()
        keep.wait()

    pl.semaphore_wait(barrier, 70)

    def far_copy(i):
        return pltpu.make_async_remote_copy(
            own, own, z_send.at[i - 1], z_recv.at[half],
            device_id=at((z + 4 * i) % 16, y), device_id_type=MESH,
        )

    def near_copy(which, step):
        block = duals.at[y, which]
        return pltpu.make_async_remote_copy(
            block, block, near_send.at[which, step], z_recv.at[which],
            device_id=at((z + (1, 2, 15)[step]) % 16, y), device_id_type=MESH,
        )

    def y_copy(which, i):
        block = duals.at[y, which]
        return pltpu.make_async_remote_copy(
            block, block, y_send.at[which, i - 1], y_recv.at[which, i - 1],
            device_id=at(z, (y + i) % 4), device_id_type=MESH,
        )

    def prop_copy(i):
        return pltpu.make_async_remote_copy(
            prop_in, prop_out, prop_send.at[i - 1], prop_recv,
            device_id=to((chol + i) % 8, walk), device_id_type=MESH,
        )

    @pl.when(computes)
    def _():
        for i in (2, 1, 3):
            far_copy(i).start()

    def settle(which):
        block = duals.at[y, which]

        @pl.when(jnp.logical_not(jnp.logical_and(computes, half == which)))
        def _():
            pltpu.make_async_copy(block, block, z_recv.at[which]).wait()

        @pl.when(hub)
        def _():
            for step in range(3):
                near_copy(which, step).start()

        for i in (1, 3, 2):
            y_copy(which, i).start()

    settle(half)
    settle(1 - half)

    @pl.when(computes)
    def _():
        pltpu.make_async_copy(prop_in, prop_out, prop_recv).start()
        for i in range(1, 8):
            prop_copy(i).start()

    load_rall.wait()

    def pair_energy(yy):
        block = jnp.concatenate([duals[yy, 0], duals[yy, 1]], axis=1)
        flipped = jnp.transpose(block)

        def vectors(i, carry):
            first, second = carry
            rows = rall[pl.ds(pl.multiple_of(i * 256, 256), 256), :]
            products = jnp.dot(rows, block, preferred_element_type=jnp.float32)
            swapped = lax.dot_general(
                flipped, rows, (((1,), (1,)), ((), ())), preferred_element_type=jnp.float32
            )
            for g in (0, 128):
                one = products[g : g + 128, 0:128] * swapped[0:128, g : g + 128]
                two = products[g : g + 128, 128:256] * swapped[128:256, g : g + 128]
                first = first + jnp.sum(one.reshape(16, 8, 128), axis=0)
                second = second + jnp.sum(two.reshape(16, 8, 128), axis=0)
            return first, second

        zero = jnp.zeros((8, 128), jnp.float32)
        first, second = lax.fori_loop(0, 16, vectors, (zero, zero))
        pieces[yy, 0] = first
        pieces[yy, 1] = second

    def piece_copy(yy, which):
        return pltpu.make_async_remote_copy(
            pieces.at[yy, which], collected.at[z * 4 + y], piece_send.at[yy, which], piece_recv,
            device_id=at(which * 8 + 2 * x + yy // 2, yy), device_id_type=MESH,
        )

    def is_me(yy, which):
        return jnp.logical_and(yy == y, z == which * 8 + 2 * x + yy // 2)

    def send_piece(yy, which):
        @pl.when(jnp.logical_not(is_me(yy, which)))
        def _():
            piece_copy(yy, which).start()

        @pl.when(is_me(yy, which))
        def _():
            pltpu.make_async_copy(
                pieces.at[yy, which], collected.at[z * 4 + y], piece_recv
            ).start()

    def each_pair(i, carry):
        yy = (y + 4 - i) % 4

        @pl.when(i > 0)
        def _():
            for which in (0, 1):
                block = duals.at[yy, which]
                pltpu.make_async_copy(block, block, y_recv.at[which, i - 1]).wait()

        pair_energy(yy)
        for which in (0, 1):
            send_piece(yy, which)
        return carry

    lax.fori_loop(0, 4, each_pair, 0)

    def final_copy(i):
        return pltpu.make_async_remote_copy(
            answer.at[0], answer.at[1], final_send.at[i - 1], final_recv,
            device_id=to((chol + i) % 8, walk), device_id_type=MESH,
        )

    @pl.when(computes)
    def _():
        pltpu.make_async_copy(collected, collected, piece_recv).wait()
        lanes = jnp.sum(jnp.sum(collected[...], axis=0), axis=0, keepdims=True)
        value = -0.5 * jnp.sum(lanes, axis=1, keepdims=True)
        answer[0] = jnp.broadcast_to(value, (8, 128))
        for i in range(1, 8):
            final_copy(i).start()
        pltpu.make_async_copy(answer.at[0], answer.at[1], final_recv).start()

    pltpu.make_async_copy(answer.at[1], answer.at[1], final_recv).wait()
    energy_out[...] = answer[1]
    pltpu.make_async_copy(prop_out, prop_out, prop_recv).wait()

    @pl.when(computes)
    def _():
        for i in (1, 2, 3):
            far_copy(i).wait_send()
        for i in range(1, 8):
            prop_copy(i).wait_send()
            final_copy(i).wait_send()

    @pl.when(hub)
    def _():
        for which in (0, 1):
            for step in range(3):
                near_copy(which, step).wait_send()

    for which in (0, 1):
        for i in (1, 2, 3):
            y_copy(which, i).wait_send()
        for yy in range(4):

            @pl.when(jnp.logical_not(is_me(yy, which)))
            def _():
                piece_copy(yy, which).wait_send()


def energy(propagated, dual, rotated):
    any_ref = pl.BlockSpec(memory_space=pl.ANY)
    vmem = pl.BlockSpec(memory_space=VMEM)
    return pl.pallas_call(
        energy_kernel,
        out_shape=(
            jax.ShapeDtypeStruct((ORB, OCC), jnp.float32),
            jax.ShapeDtypeStruct((8, 128), jnp.float32),
        ),
        in_specs=[vmem, vmem, any_ref],
        out_specs=(vmem, vmem),
        scratch_shapes=[
            VMEM((4096, ORB), jnp.bfloat16),
            VMEM((4, 2, ORB, OCC), jnp.bfloat16),
            VMEM((4, 2, 8, 128), jnp.float32),
            VMEM((64, 8, 128), jnp.float32),
            VMEM((2, 8, 128), jnp.float32),
            DMA, DMA, DMA, DMA((3,)), DMA((2, 3)), DMA((2,)), DMA((2, 3)), DMA((2, 3)),
            DMA((7,)), DMA, DMA((4, 2)), DMA, DMA((7,)), DMA,
        ],
        compiler_params=pltpu.CompilerParams(collective_id=1, has_side_effects=True),
        name="energy",
    )(propagated, dual, rotated)


def per_device(field_draws, chol_vectors, rotated_vectors, walkers):
    operator, rotated = gather(
        field_draws.astype(jnp.float32),
        chol_vectors.reshape(256 * 8, ORB),
        rotated_vectors.reshape(512, ORB),
    )
    propagated, dual = propagate(operator.reshape(ORB, ORB), walkers.reshape(ORB, OCC))
    propagated, exchange = energy(propagated, dual, rotated.reshape(4096, ORB))
    return (propagated.reshape(1, ORB, OCC), exchange[0, 0:1])


def solution(mesh):
    return jax.shard_map(
        per_device,
        mesh=mesh,
        in_specs=(
            P("walk", "chol"),
            P("chol", "walk", None),
            P(("chol", "walk"), None, None),
            P("walk", None, None),
        ),
        out_specs=(P("walk", None, None), P("walk")),
        check_vma=False,
    )
```

time: 558 us -> 147 us (0.26)
  the two profiles are of different devices: /device:TPU:1 before, /device:TPU:96 now
where the time goes in v1:
time: 147 us
  Pallas kernels  142 us (97%)
  local copies, waits for them, and re-layouts  2.85 us (2%)
    pallas_call x1, Pallas kernels, energy(): pl.pallas_call(energy_kernel, out_shape=(jax.ShapeDtypeStruct((ORB, OCC),...  72.2 us
    pallas_call x1, Pallas kernels, gather(): pl.pallas_call(gather_kernel, out_shape=(jax.ShapeDtypeStruct((SLABS, 8,...  53.7 us
    pallas_call x1, Pallas kernels, propagate(): pl.pallas_call(propagate_kernel, out_shape=(jax.ShapeDtypeStruct((ORB, OC...  16.5 us

profile of v1, /device:TPU:96, one launch (start us, length us, event | category | flops | bytes accessed | tf_op | source)
XLA Modules:
  0.0 147.2 jit_solution(12026008124935451018)
XLA Ops:
  0.6 1.2 convert_element_type.3.draws_ref
  1.9 53.7 %gather.1 = (bf16[64,8,512]{2,1,0:T(8,128)(2,1)}, bf16[4,2,512,512]{3,2,1,0:T(8,128)(2,1)}) custom-call(f32[1,256]{1,0:T(1,128)} %convert_element_type.3.draws_ref, bf16[2048,512]{1,0:T(8,128)(2,1)} %bitcast.8, bf16[512,512]{1,0:T(8,128)(2,1)} %bitcast.9), custom_call_target="tpu_custom_call" | custom-call | tf_op jit(solution)/shard_map/gather/pallas_call | solution.py:193
  55.6 16.5 %propagate.1 = (f32[512,128]{1,0:T(8,128)}, bf16[512,128]{1,0:T(8,128)(2,1)}) custom-call(bf16[512,512]{1,0:T(8,128)(2,1)} %bitcast.10, bf16[512,128]{1,0:T(8,128)(2,1)} %bitcast.12), custom_call_target="tpu_custom_call" | custom-call | tf_op jit(solution)/shard_map/propagate/pallas_call | solution.py:253
  72.1 72.2 %energy.1 = (f32[512,128]{1,0:T(8,128)}, f32[8,128]{1,0:T(8,128)}) custom-call(f32[512,128]{1,0:T(8,128)} %get-tuple-element.9.prop_in, bf16[512,128]{1,0:T(8,128)(2,1)} %get-tuple-element.10.dual_in, bf16[4096,512]{1,0:T(8,128)(2,1)} %bitcast.7), custom_call_target="tpu_custom_call" | custom-call | tf_op jit(solution)/shard_map/energy/pallas_call | solution.py:469
  144.3 1.2 slice.3
  145.5 1.7 %copy.7 = f32[1,512,128]{2,1,0:T(8,128)} copy(f32[1,512,128]{2,1,0:T(8,128)} %bitcast.11) | data formatting | bytes 524288

commit v2 on v0

v2 whole, which is shorter than its diff:
```python
import functools

import jax
import jax.numpy as jnp
from jax import lax
from jax.experimental import pallas as pl
from jax.experimental.pallas import tpu as pltpu
from jax.sharding import PartitionSpec as P

ORB = 512
OCC = 128
TERMS = 4
SLABS = 64
CHOL = 8
MESH = pl.DeviceIdType.MESH
HIGHEST = lax.Precision.HIGHEST
VMEM = pltpu.VMEM
DMA = pltpu.SemaphoreType.DMA


def here():
    chol = lax.axis_index("chol")
    walk = lax.axis_index("walk")
    return chol, walk


def to(chol, walk):
    return {"chol": chol, "walk": walk}


def invert(corr):
    lane = lax.broadcasted_iota(jnp.int32, (OCC, OCC), 1)
    sub = lax.broadcasted_iota(jnp.int32, (OCC, OCC), 0)
    column_sub = lax.broadcasted_iota(jnp.int32, (OCC, 1), 0)
    row_lane = lax.broadcasted_iota(jnp.int32, (4, OCC), 1)
    row_sub = lax.broadcasted_iota(jnp.int32, (4, OCC), 0)

    def pair_inverse(m):
        (a, b), (c, d) = m
        scale = 1.0 / (a * d - b * c)
        return ((d * scale, -b * scale), (-c * scale, a * scale))

    def mul(m, n):
        return tuple(
            tuple(m[i][0] * n[0][j] + m[i][1] * n[1][j] for j in (0, 1)) for i in (0, 1)
        )

    def add(m, n, sign):
        return tuple(tuple(m[i][j] + sign * n[i][j] for j in (0, 1)) for i in (0, 1))

    def eliminate(k, carry):
        base = k * 4
        full = corr[...]
        panel = corr[pl.ds(base, 4), :]
        columns = [
            jnp.sum(jnp.where(lane == base + j, full, 0.0), axis=1, keepdims=True) for j in range(4)
        ]
        heads = [
            jnp.sum(jnp.where(row_lane == base + j, panel, 0.0), axis=1, keepdims=True)
            for j in range(4)
        ]

        def block(i, j):
            return tuple(
                tuple(heads[2 * j + b][2 * i + a : 2 * i + a + 1, :] for b in (0, 1)) for a in (0, 1)
            )

        top = pair_inverse(block(0, 0))
        right = mul(top, block(0, 1))
        left = mul(block(1, 0), top)
        low = pair_inverse(add(block(1, 1), mul(block(1, 0), right), -1.0))
        low_left = mul(low, left)
        corner = add(top, mul(right, low_left), 1.0)
        high_right = mul(right, low)
        inverse = (
            corner[0] + tuple(-v for v in high_right[0]),
            corner[1] + tuple(-v for v in high_right[1]),
            tuple(-v for v in low_left[0]) + low[0],
            tuple(-v for v in low_left[1]) + low[1],
        )
        in_pivot = jnp.logical_and(row_lane >= base, row_lane < base + 4)
        panel = jnp.where(in_pivot, jnp.where(row_lane == base + row_sub, 1.0, 0.0), panel)
        result = jnp.where(
            jnp.logical_or(
                jnp.logical_and(lane >= base, lane < base + 4),
                jnp.logical_and(sub >= base, sub < base + 4),
            ),
            0.0,
            full,
        )
        pivot_rows = jnp.logical_and(column_sub >= base, column_sub < base + 4)
        for j in range(4):
            scaled = inverse[j][0] * panel[0:1, :]
            for m in range(1, 4):
                scaled = scaled + inverse[j][m] * panel[m : m + 1, :]
            unit = jnp.where(column_sub == base + j, -1.0, 0.0)
            result = result - jnp.where(pivot_rows, unit, columns[j]) * scaled
        corr[...] = result
        return carry

    lax.fori_loop(0, OCC // 4, eliminate, 0)


def step_kernel(
    draws_ref, chol_hbm, rot_hbm, walker_ref, prop_out, energy_out,
    chol_buf, draw_row, gathered, acc, part, recv, red, oper, rall, prop, corr, duals,
    pieces, collected, answer,
    chol_sem, rot_sem, draw_send, draw_recv, part_send, part_recv,
    row_send, row_recv, x_send, x_recv, sib_send, sib_recv,
    z_send, z_recv, y_send, y_recv, prop_send, prop_recv,
    piece_send, piece_recv, final_send, final_recv,
):
    chol, walk = here()
    z = walk // 4
    core = walk % 2
    x = chol // 2
    y_hi = chol % 2
    y = y_hi * 2 + (walk // 2) % 2
    sibling = walk + 1 - 2 * core
    computes = (z % 8) == chol
    barrier = pltpu.get_barrier_semaphore()

    def remote(src, dst, send, recv_sem, device):
        return pltpu.make_async_remote_copy(
            src, dst, send, recv_sem, device_id=device, device_id_type=MESH
        )

    def at(zz, yy):
        return to(x * 2 + yy // 2, zz * 4 + (yy % 2) * 2 + core)

    def greet(device):
        pl.semaphore_signal(barrier, inc=1, device_id=device, device_id_type=MESH)

    def greet_walk(i, carry):
        greet(to(chol, (walk + i) % 64))
        return carry

    def greet_plane(i, carry):
        greet(to(x * 2 + 1 - y_hi, i * 2 + core))
        return carry

    def greet_chol(i, carry):
        greet(to((chol + i) % 8, walk))
        return carry

    lax.fori_loop(1, 64, greet_walk, 0)
    lax.fori_loop(1, 8, greet_chol, 0)
    lax.fori_loop(0, 32, greet_plane, 0)
    load_chol = pltpu.make_async_copy(chol_hbm, chol_buf, chol_sem)
    load_chol.start()
    load_rot = pltpu.make_async_copy(rot_hbm, rall.at[x, core], rot_sem)
    load_rot.start()
    draw_row[...] = draws_ref[...].astype(jnp.float32)
    slot = (z % 8) * 8 + (z // 8) * 4 + walk % 4
    pl.semaphore_wait(barrier, 63 + 7 + 32)

    own_draw = pltpu.make_async_copy(draw_row, gathered.at[slot], draw_recv)
    own_draw.start()

    def send_draw(i, carry):
        remote(
            draw_row, gathered.at[slot], draw_send, draw_recv, to(chol, (walk + i) % 64)
        ).start()
        return carry

    lax.fori_loop(1, 64, send_draw, 0)

    load_rot.wait()

    def x_copy(i):
        mine = rall.at[x, core]
        return remote(
            mine, mine, x_send.at[i - 1], x_recv.at[i - 1], to(((x + i) % 4) * 2 + y_hi, walk)
        )

    def sib_copy(i):
        block = rall.at[(x + 4 - i) % 4, core]
        return remote(block, block, sib_send.at[i], sib_recv.at[i], to(chol, sibling))

    x_copy(1).start()
    x_copy(3).start()
    sib_copy(0).start()

    load_chol.wait()
    pltpu.make_async_copy(gathered, gathered, draw_recv).wait()

    draws = gathered[...].reshape(SLABS, 256)
    draws = jnp.broadcast_to(draws[:, None, :], (SLABS, 8, 256))
    draws = draws.reshape(SLABS * 8, 256).astype(jnp.bfloat16)
    same_row = (lax.broadcasted_iota(jnp.int32, (512, 256), 0) % 8) == (
        lax.broadcasted_iota(jnp.int32, (512, 256), 1) % 8
    )
    vec_iota = lax.broadcasted_iota(jnp.int32, (256, 256), 0)
    col_iota = lax.broadcasted_iota(jnp.int32, (256, 256), 1) // 8
    acc[...] = jnp.zeros_like(acc)

    def chunk(i, carry):
        pick = jnp.where(vec_iota == col_iota + i * 32, 1.0, 0.0).astype(jnp.bfloat16)
        spread = jnp.dot(draws, pick, preferred_element_type=jnp.float32)
        spread = jnp.where(same_row, spread, 0.0).astype(jnp.bfloat16)
        rows = pl.ds(pl.multiple_of(i * 256, 256), 256)
        acc[...] += jnp.dot(spread, chol_buf[rows, :], preferred_element_type=jnp.float32)
        return carry

    lax.fori_loop(0, 8, chunk, 0)
    for peer in range(CHOL):
        part[peer] = acc[peer * 64 : peer * 64 + 64, :].astype(jnp.bfloat16)

    def part_copy(i):
        peer = (chol + i) % 8
        return remote(
            part.at[peer], recv.at[i - 1], part_send.at[i - 1], part_recv.at[i - 1], to(peer, walk)
        )

    for i in range(1, 8):
        part_copy(i).start()
    total = acc[pl.ds(pl.multiple_of(chol * 64, 64), 64), :]
    for i in range(1, 8):
        part_copy(i).wait_recv()
        total = total + recv[i - 1].astype(jnp.float32)
    red[...] = total.astype(jnp.bfloat16).reshape(8, 8, ORB)

    def row_target(j):
        return ((j // 4) * 8 + chol) * 4 + j % 4

    def row_copy(j):
        return remote(
            red.at[j], oper.at[walk], row_send.at[j], row_recv, to(chol, row_target(j))
        )

    def send_rows(j, carry):
        @pl.when(row_target(j) != walk)
        def _():
            row_copy(j).start()

        @pl.when(row_target(j) == walk)
        def _():
            pltpu.make_async_copy(red.at[j], oper.at[walk], row_recv).start()

        return carry

    lax.fori_loop(0, 8, send_rows, 0)
    x_copy(2).start()
    for i in (1, 3):
        x_copy(i).wait_recv()
        sib_copy(i).start()

    @pl.when(computes)
    def _():
        pltpu.make_async_copy(oper, oper, row_recv).wait()
        walker = walker_ref[...]
        term = walker
        summed = walker.astype(jnp.float32)
        operator = oper[...].reshape(ORB, ORB)
        for degree in range(1, TERMS + 1):
            applied = jnp.dot(operator, term, preferred_element_type=jnp.float32)
            term = (applied / degree).astype(jnp.bfloat16)
            summed = summed + term.astype(jnp.float32)
        prop[...] = summed
        corr[...] = lax.dot_general(
            walker.astype(jnp.float32), summed, (((0,), (0,)), ((), ())), precision=HIGHEST,
            preferred_element_type=jnp.float32,
        )
        invert(corr)
        duals[y, z // 8] = jnp.dot(
            prop[...], corr[...], precision=HIGHEST, preferred_element_type=jnp.float32
        ).astype(jnp.bfloat16)

    def hop(which, kind):
        block = duals.at[y, which]
        return remote(
            block, block, z_send.at[which, kind], z_recv.at[which],
            at((z + (4, 12, 1, 15)[kind]) % 16, y),
        )

    def away(which):
        return (z + 16 - which * 8 - chol) % 16

    def any_of(value, options):
        found = value == options[0]
        for option in options[1:]:
            found = jnp.logical_or(found, value == option)
        return found

    def hops(which):
        d = away(which)
        return (
            jnp.logical_or(d == 0, jnp.logical_and(d == 4, core == 0)),
            jnp.logical_or(d == 0, jnp.logical_and(d == 12, core == 1)),
            any_of(d, (0, 1, 4, 5, 8, 12)),
            any_of(d, (0, 15, 4, 12, 11, 8)),
        )

    def y_copy(which, i):
        block = duals.at[y, which]
        return remote(
            block, block, y_send.at[which, i - 1], y_recv.at[which, i - 1], at(z, (y + i) % 4)
        )

    step = 1 + 2 * core

    def y_relay(which):
        block = duals.at[(y + 4 - step) % 4, which]
        return remote(
            block, block, y_send.at[which, 1], y_recv.at[which, 1], at(z, (y + step) % 4)
        )

    def settle(which):
        block = duals.at[y, which]

        @pl.when(away(which) != 0)
        def _():
            pltpu.make_async_copy(block, block, z_recv.at[which]).wait()

        for kind, condition in enumerate(hops(which)):

            @pl.when(condition)
            def _():
                hop(which, kind).start()

        y_copy(which, 1).start()
        y_copy(which, 3).start()

    def pass_on(which):
        block = duals.at[(y + 4 - step) % 4, which]
        pltpu.make_async_copy(block, block, y_recv.at[which, step - 1]).wait()
        y_relay(which).start()

    d = away(0)
    first = jnp.where(jnp.logical_or(d <= 4, d >= 12), 0, 1)
    settle(first)
    x_copy(2).wait_recv()
    sib_copy(2).start()
    pass_on(first)
    settle(1 - first)
    pass_on(1 - first)

    def prop_copy(i):
        return remote(prop, prop_out, prop_send.at[i - 1], prop_recv, to((chol + i) % 8, walk))

    @pl.when(computes)
    def _():
        for i in range(1, 8):
            prop_copy(i).start()
        pltpu.make_async_copy(prop, prop_out, prop_recv).start()

    for i in range(4):
        sib_copy(i).wait_recv()

    def pair_energy(yy):
        block = jnp.concatenate([duals[yy, 0], duals[yy, 1]], axis=1)
        flipped = jnp.transpose(block)

        def vectors(i, carry):
            one_sum, two_sum = carry
            rows = rall[i // 4, (i // 2) % 2, pl.ds(pl.multiple_of((i % 2) * 256, 256), 256), :]
            products = jnp.dot(rows, block, preferred_element_type=jnp.float32)
            swapped = lax.dot_general(
                flipped, rows, (((1,), (1,)), ((), ())), preferred_element_type=jnp.float32
            )
            for g in (0, 128):
                one = products[g : g + 128, 0:128] * swapped[0:128, g : g + 128]
                two = products[g : g + 128, 128:256] * swapped[128:256, g : g + 128]
                one_sum = one_sum + jnp.sum(one.reshape(16, 8, 128), axis=0)
                two_sum = two_sum + jnp.sum(two.reshape(16, 8, 128), axis=0)
            return one_sum, two_sum

        zero = jnp.zeros((8, 128), jnp.float32)
        one_sum, two_sum = lax.fori_loop(0, 16, vectors, (zero, zero))
        pieces[yy, 0] = one_sum
        pieces[yy, 1] = two_sum

    def piece_copy(yy, which):
        return remote(
            pieces.at[yy, which], collected.at[z * 4 + y], piece_send.at[yy, which], piece_recv,
            at(which * 8 + 2 * x + yy // 2, yy),
        )

    def is_me(yy, which):
        return jnp.logical_and(yy == y, z == which * 8 + 2 * x + yy // 2)

    def send_piece(yy, which):
        @pl.when(jnp.logical_not(is_me(yy, which)))
        def _():
            piece_copy(yy, which).start()

        @pl.when(is_me(yy, which))
        def _():
            pltpu.make_async_copy(
                pieces.at[yy, which], collected.at[z * 4 + y], piece_recv
            ).start()

    def each_pair(n, carry):
        i = jnp.where(n == 2, 3, jnp.where(n == 3, 2, n))
        yy = (y + 4 - i) % 4

        @pl.when(jnp.logical_and(n > 0, i != step))
        def _():
            for which in (0, 1):
                block = duals.at[yy, which]
                pltpu.make_async_copy(block, block, y_recv.at[which, i - 1]).wait()

        pair_energy(yy)
        for which in (0, 1):
            send_piece(yy, which)
        return carry

    lax.fori_loop(0, 4, each_pair, 0)

    def final_copy(i):
        return remote(
            answer.at[0], answer.at[1], final_send.at[i - 1], final_recv, to((chol + i) % 8, walk)
        )

    @pl.when(computes)
    def _():
        pltpu.make_async_copy(collected, collected, piece_recv).wait()
        lanes = jnp.sum(jnp.sum(collected[...], axis=0), axis=0, keepdims=True)
        value = -0.5 * jnp.sum(lanes, axis=1, keepdims=True)
        answer[0] = jnp.broadcast_to(value, (8, 128))
        for i in range(1, 8):
            final_copy(i).start()
        pltpu.make_async_copy(answer.at[0], answer.at[1], final_recv).start()

    def drain_rows(j, carry):
        @pl.when(row_target(j) != walk)
        def _():
            row_copy(j).wait_send()

        return carry

    lax.fori_loop(0, 8, drain_rows, 0)
    sent = gathered.at[pl.ds(0, 63)]
    pltpu.make_async_copy(sent, sent, draw_send).wait()
    for i in range(1, 8):
        part_copy(i).wait_send()
    for i in (1, 2, 3):
        x_copy(i).wait_send()
    for i in range(4):
        sib_copy(i).wait_send()
    for which in (0, 1):
        for kind, condition in enumerate(hops(which)):

            @pl.when(condition)
            def _():
                hop(which, kind).wait_send()

        y_copy(which, 1).wait_send()
        y_copy(which, 3).wait_send()
        y_relay(which).wait_send()
        for yy in range(4):

            @pl.when(jnp.logical_not(is_me(yy, which)))
            def _():
                piece_copy(yy, which).wait_send()

    pltpu.make_async_copy(prop_out, prop_out, prop_recv).wait()

    @pl.when(computes)
    def _():
        for i in range(1, 8):
            prop_copy(i).wait_send()
            final_copy(i).wait_send()

    pltpu.make_async_copy(answer.at[1], answer.at[1], final_recv).wait()
    energy_out[...] = answer[1]


def per_device(field_draws, chol_vectors, rotated_vectors, walkers):
    any_ref = pl.BlockSpec(memory_space=pl.ANY)
    vmem = pl.BlockSpec(memory_space=VMEM)
    propagated, exchange = pl.pallas_call(
        step_kernel,
        out_shape=(
            jax.ShapeDtypeStruct((ORB, OCC), jnp.float32),
            jax.ShapeDtypeStruct((8, 128), jnp.float32),
        ),
        in_specs=[vmem, any_ref, any_ref, vmem],
        out_specs=(vmem, vmem),
        scratch_shapes=[
            VMEM((2048, ORB), jnp.bfloat16),
            VMEM((1, 256), jnp.float32),
            VMEM((SLABS, 1, 256), jnp.float32),
            VMEM((512, ORB), jnp.float32),
            VMEM((CHOL, 64, ORB), jnp.bfloat16),
            VMEM((CHOL - 1, 64, ORB), jnp.bfloat16),
            VMEM((8, 8, ORB), jnp.bfloat16),
            VMEM((SLABS, 8, ORB), jnp.bfloat16),
            VMEM((4, 2, 512, ORB), jnp.bfloat16),
            VMEM((ORB, OCC), jnp.float32),
            VMEM((OCC, OCC), jnp.float32),
            VMEM((4, 2, ORB, OCC), jnp.bfloat16),
            VMEM((4, 2, 8, 128), jnp.float32),
            VMEM((64, 8, 128), jnp.float32),
            VMEM((2, 8, 128), jnp.float32),
            DMA, DMA, DMA, DMA, DMA((7,)), DMA((7,)),
            DMA((8,)), DMA, DMA((3,)), DMA((3,)), DMA((4,)), DMA((4,)),
            DMA((2, 4)), DMA((2,)), DMA((2, 3)), DMA((2, 3)), DMA((7,)), DMA,
            DMA((4, 2)), DMA, DMA((7,)), DMA,
        ],
        compiler_params=pltpu.CompilerParams(collective_id=0, has_side_effects=True),
        name="step",
    )(
        field_draws,
        chol_vectors.reshape(256 * 8, ORB),
        rotated_vectors.reshape(512, ORB),
        walkers.reshape(ORB, OCC),
    )
    return (propagated.reshape(1, ORB, OCC), exchange[0, 0:1])


def solution(mesh):
    return jax.shard_map(
        per_device,
        mesh=mesh,
        in_specs=(
            P("walk", "chol"),
            P("chol", "walk", None),
            P(("chol", "walk"), None, None),
            P("walk", None, None),
        ),
        out_specs=(P("walk", None, None), P("walk")),
        check_vma=False,
    )
```

time: 558 us -> 145 us (0.26)
  the two profiles are of different devices: /device:TPU:1 before, /device:TPU:36 now
where the time goes in v2:
time: 145 us; the launch traced here: 144 us
  Pallas kernels  141 us (97%)
  local copies, waits for them, and re-layouts  2.86 us (2%)
    pallas_call x1, Pallas kernels, per_device(): pl.pallas_call(step_kernel, out_shape=(jax.ShapeDtypeStruct((ORB, OCC), j...  141 us

profile of v2, /device:TPU:36, one launch (start us, length us, event | category | flops | bytes accessed | tf_op | source)
XLA Modules:
  0.0 144.5 jit_solution(11803121808425070714)
XLA Ops:
  0.6 140.9 %step.1 = (f32[512,128]{1,0:T(8,128)}, f32[8,128]{1,0:T(8,128)}) custom-call(bf16[1,256]{1,0:T(2,128)(2,1)} %draws_ref.1, bf16[2048,512]{1,0:T(8,128)(2,1)} %bitcast.5, bf16[512,512]{1,0:T(8,128)(2,1)} %bitcast.6, bf16[512,128]{1,0:T(8,128)(2,1)} %bitcast.8), custom_call_target="tpu_custom_call" | custom-call | tf_op jit(solution)/shard_map/step/pallas_call | solution.py:472
  141.6 1.2 slice.3
  142.8 1.7 %copy.7 = f32[1,512,128]{2,1,0:T(8,128)} copy(f32[1,512,128]{2,1,0:T(8,128)} %bitcast.7) | data formatting | bytes 524288

commit v3 on v2

--- a/solution.py
+++ b/solution.py
@@ -29,11 +29,8 @@
 
 
 def invert(corr):
-    lane = lax.broadcasted_iota(jnp.int32, (OCC, OCC), 1)
-    sub = lax.broadcasted_iota(jnp.int32, (OCC, OCC), 0)
-    column_sub = lax.broadcasted_iota(jnp.int32, (OCC, 1), 0)
-    row_lane = lax.broadcasted_iota(jnp.int32, (4, OCC), 1)
-    row_sub = lax.broadcasted_iota(jnp.int32, (4, OCC), 0)
+    lane = lax.broadcasted_iota(jnp.int32, (8, OCC), 1)
+    sub = lax.broadcasted_iota(jnp.int32, (8, OCC), 0)
 
     def pair_inverse(m):
         (a, b), (c, d) = m
@@ -48,21 +45,21 @@
     def add(m, n, sign):
         return tuple(tuple(m[i][j] + sign * n[i][j] for j in (0, 1)) for i in (0, 1))
 
-    def eliminate(k, carry):
-        base = k * 4
-        full = corr[...]
-        panel = corr[pl.ds(base, 4), :]
+    def pivots(full, p):
         columns = [
-            jnp.sum(jnp.where(lane == base + j, full, 0.0), axis=1, keepdims=True) for j in range(4)
-        ]
-        heads = [
-            jnp.sum(jnp.where(row_lane == base + j, panel, 0.0), axis=1, keepdims=True)
+            jnp.broadcast_to(full[:, p + j : p + j + 1], (OCC, OCC)).reshape(16, 8, OCC)
             for j in range(4)
         ]
 
         def block(i, j):
             return tuple(
-                tuple(heads[2 * j + b][2 * i + a : 2 * i + a + 1, :] for b in (0, 1)) for a in (0, 1)
+                tuple(
+                    jnp.broadcast_to(
+                        columns[2 * j + b][0, p + 2 * i + a : p + 2 * i + a + 1, :], (8, OCC)
+                    )
+                    for b in (0, 1)
+                )
+                for a in (0, 1)
             )
 
         top = pair_inverse(block(0, 0))
@@ -78,32 +75,37 @@
             tuple(-v for v in low_left[0]) + low[0],
             tuple(-v for v in low_left[1]) + low[1],
         )
-        in_pivot = jnp.logical_and(row_lane >= base, row_lane < base + 4)
-        panel = jnp.where(in_pivot, jnp.where(row_lane == base + row_sub, 1.0, 0.0), panel)
-        result = jnp.where(
-            jnp.logical_or(
-                jnp.logical_and(lane >= base, lane < base + 4),
-                jnp.logical_and(sub >= base, sub < base + 4),
-            ),
-            0.0,
-            full,
-        )
-        pivot_rows = jnp.logical_and(column_sub >= base, column_sub < base + 4)
+        in_pivot = jnp.logical_and(lane >= p, lane < p + 4)
+        rows = []
+        for m in range(4):
+            row = jnp.broadcast_to(full[p + m : p + m + 1, :], (8, OCC))
+            rows.append(jnp.where(in_pivot, jnp.where(lane == p + m, 1.0, 0.0), row))
+        result = jnp.where(in_pivot[None], 0.0, full.reshape(16, 8, OCC))
+        scaled = []
         for j in range(4):
-            scaled = inverse[j][0] * panel[0:1, :]
+            line = inverse[j][0] * rows[0]
             for m in range(1, 4):
-                scaled = scaled + inverse[j][m] * panel[m : m + 1, :]
-            unit = jnp.where(column_sub == base + j, -1.0, 0.0)
-            result = result - jnp.where(pivot_rows, unit, columns[j]) * scaled
-        corr[...] = result
-        return carry
-
-    lax.fori_loop(0, OCC // 4, eliminate, 0)
+                line = line + inverse[j][m] * rows[m]
+            scaled.append(line)
+            result = result - columns[j] * line[None]
+        head = result[0]
+        for j in range(4):
+            head = jnp.where(sub == p + j, scaled[j], head)
+        return jnp.concatenate([head, result[1:].reshape(OCC - 8, OCC)], axis=0)
+
+    def eliminate(k, carry):
+        full = pivots(pivots(corr[...], 0), 4)
+        full = pltpu.roll(full, OCC - 8, 1)
+        corr[0 : OCC - 8, :] = full[8:, :]
+        corr[OCC - 8 :, :] = full[0:8, :]
+        return carry
+
+    lax.fori_loop(0, OCC // 8, eliminate, 0)
 
 
 def step_kernel(
     draws_ref, chol_hbm, rot_hbm, walker_ref, prop_out, energy_out,
-    chol_buf, draw_row, gathered, acc, part, recv, red, oper, rall, prop, corr, duals,
+    chol_buf, draw_row, gathered, spreads, acc, part, recv, red, oper, rall, prop, corr, duals,
     pieces, collected, answer,
     chol_sem, rot_sem, draw_send, draw_recv, part_send, part_recv,
     row_send, row_recv, x_send, x_recv, sib_send, sib_recv,
@@ -192,33 +194,37 @@
     )
     vec_iota = lax.broadcasted_iota(jnp.int32, (256, 256), 0)
     col_iota = lax.broadcasted_iota(jnp.int32, (256, 256), 1) // 8
-    acc[...] = jnp.zeros_like(acc)
 
     def chunk(i, carry):
         pick = jnp.where(vec_iota == col_iota + i * 32, 1.0, 0.0).astype(jnp.bfloat16)
         spread = jnp.dot(draws, pick, preferred_element_type=jnp.float32)
-        spread = jnp.where(same_row, spread, 0.0).astype(jnp.bfloat16)
-        rows = pl.ds(pl.multiple_of(i * 256, 256), 256)
-        acc[...] += jnp.dot(spread, chol_buf[rows, :], preferred_element_type=jnp.float32)
+        columns = pl.ds(pl.multiple_of(i * 256, 256), 256)
+        spreads[:, columns] = jnp.where(same_row, spread, 0.0).astype(jnp.bfloat16)
         return carry
 
     lax.fori_loop(0, 8, chunk, 0)
-    for peer in range(CHOL):
-        part[peer] = acc[peer * 64 : peer * 64 + 64, :].astype(jnp.bfloat16)
-
-    def part_copy(i):
+
+    def part_copy(n, i):
         peer = (chol + i) % 8
         return remote(
-            part.at[peer], recv.at[i - 1], part_send.at[i - 1], part_recv.at[i - 1], to(peer, walk)
-        )
-
-    for i in range(1, 8):
-        part_copy(i).start()
-    total = acc[pl.ds(pl.multiple_of(chol * 64, 64), 64), :]
-    for i in range(1, 8):
-        part_copy(i).wait_recv()
-        total = total + recv[i - 1].astype(jnp.float32)
-    red[...] = total.astype(jnp.bfloat16).reshape(8, 8, ORB)
+            part.at[n, peer], recv.at[n, i - 1], part_send.at[n, i - 1], part_recv.at[n, i - 1],
+            to(peer, walk),
+        )
+
+    for n in range(2):
+        terms = jnp.dot(
+            spreads[...], chol_buf[:, n * 256 : n * 256 + 256], preferred_element_type=jnp.float32
+        )
+        acc[n] = terms
+        part[n] = terms.astype(jnp.bfloat16).reshape(CHOL, 64, 256)
+        for i in range(1, 8):
+            part_copy(n, i).start()
+    for n in range(2):
+        total = acc[n, pl.ds(pl.multiple_of(chol * 64, 64), 64), :]
+        for i in range(1, 8):
+            part_copy(n, i).wait_recv()
+            total = total + recv[n, i - 1].astype(jnp.float32)
+        red[:, :, n * 256 : n * 256 + 256] = total.astype(jnp.bfloat16).reshape(8, 8, 256)
 
     def row_target(j):
         return ((j // 4) * 8 + chol) * 4 + j % 4
@@ -329,10 +335,10 @@
     d = away(0)
     first = jnp.where(jnp.logical_or(d <= 4, d >= 12), 0, 1)
     settle(first)
+    settle(1 - first)
+    pass_on(first)
     x_copy(2).wait_recv()
     sib_copy(2).start()
-    pass_on(first)
-    settle(1 - first)
     pass_on(1 - first)
 
     def prop_copy(i):
@@ -349,26 +355,23 @@
 
     def pair_energy(yy):
         block = jnp.concatenate([duals[yy, 0], duals[yy, 1]], axis=1)
-        flipped = jnp.transpose(block)
-
-        def vectors(i, carry):
-            one_sum, two_sum = carry
-            rows = rall[i // 4, (i // 2) % 2, pl.ds(pl.multiple_of((i % 2) * 256, 256), 256), :]
+
+        def vectors(i, sums):
+            rows = rall[i].reshape(1024, ORB)
             products = jnp.dot(rows, block, preferred_element_type=jnp.float32)
-            swapped = lax.dot_general(
-                flipped, rows, (((1,), (1,)), ((), ())), preferred_element_type=jnp.float32
-            )
-            for g in (0, 128):
-                one = products[g : g + 128, 0:128] * swapped[0:128, g : g + 128]
-                two = products[g : g + 128, 128:256] * swapped[128:256, g : g + 128]
-                one_sum = one_sum + jnp.sum(one.reshape(16, 8, 128), axis=0)
-                two_sum = two_sum + jnp.sum(two.reshape(16, 8, 128), axis=0)
-            return one_sum, two_sum
+            sums = list(sums)
+            for g in range(8):
+                for w in range(2):
+                    one = products[g * 128 : g * 128 + 128, w * 128 : w * 128 + 128]
+                    swapped = jnp.transpose(one.astype(jnp.bfloat16)).astype(jnp.float32)
+                    terms = (one * swapped).reshape(16, 8, 128)
+                    sums[w] = sums[w] + jnp.sum(terms, axis=0)
+            return tuple(sums)
 
         zero = jnp.zeros((8, 128), jnp.float32)
-        one_sum, two_sum = lax.fori_loop(0, 16, vectors, (zero, zero))
-        pieces[yy, 0] = one_sum
-        pieces[yy, 1] = two_sum
+        sums = lax.fori_loop(0, 4, vectors, (zero, zero))
+        pieces[yy, 0] = sums[0]
+        pieces[yy, 1] = sums[1]
 
     def piece_copy(yy, which):
         return remote(
@@ -432,8 +435,9 @@
     lax.fori_loop(0, 8, drain_rows, 0)
     sent = gathered.at[pl.ds(0, 63)]
     pltpu.make_async_copy(sent, sent, draw_send).wait()
-    for i in range(1, 8):
-        part_copy(i).wait_send()
+    for n in range(2):
+        for i in range(1, 8):
+            part_copy(n, i).wait_send()
     for i in (1, 2, 3):
         x_copy(i).wait_send()
     for i in range(4):
@@ -481,9 +485,10 @@
             VMEM((2048, ORB), jnp.bfloat16),
             VMEM((1, 256), jnp.float32),
             VMEM((SLABS, 1, 256), jnp.float32),
-            VMEM((512, ORB), jnp.float32),
-            VMEM((CHOL, 64, ORB), jnp.bfloat16),
-            VMEM((CHOL - 1, 64, ORB), jnp.bfloat16),
+            VMEM((512, 2048), jnp.bfloat16),
+            VMEM((2, 512, 256), jnp.float32),
+            VMEM((2, CHOL, 64, 256), jnp.bfloat16),
+            VMEM((2, CHOL - 1, 64, 256), jnp.bfloat16),
             VMEM((8, 8, ORB), jnp.bfloat16),
             VMEM((SLABS, 8, ORB), jnp.bfloat16),
             VMEM((4, 2, 512, ORB), jnp.bfloat16),
@@ -493,7 +498,7 @@
             VMEM((4, 2, 8, 128), jnp.float32),
             VMEM((64, 8, 128), jnp.float32),
             VMEM((2, 8, 128), jnp.float32),
-            DMA, DMA, DMA, DMA, DMA((7,)), DMA((7,)),
+            DMA, DMA, DMA, DMA, DMA((2, 7)), DMA((2, 7)),
             DMA((8,)), DMA, DMA((3,)), DMA((3,)), DMA((4,)), DMA((4,)),
             DMA((2, 4)), DMA((2,)), DMA((2, 3)), DMA((2, 3)), DMA((7,)), DMA,
             DMA((4, 2)), DMA, DMA((7,)), DMA,

time: 145 us -> 108 us (0.74)
  Pallas kernels: 141 us -> 105 us
    pallas_call x1, Pallas kernels: 141 us -> 105 us  [per_device(): pl.pallas_call(step_kernel, out_shape=(jax.ShapeDtypeStruct((ORB, OCC), j...]
where the time goes in v3:
time: 108 us
  Pallas kernels  105 us (97%)
  local copies, waits for them, and re-layouts  2.86 us (3%)
    pallas_call x1, Pallas kernels, per_device(): pl.pallas_call(step_kernel, out_shape=(jax.ShapeDtypeStruct((ORB, OCC), j...  105 us

profile of v3, /device:TPU:36, one launch (start us, length us, event | category | flops | bytes accessed | tf_op | source)
XLA Modules:
  0.0 108.3 jit_solution(4105856157343724718)
XLA Ops:
  0.6 104.8 %step.1 = (f32[512,128]{1,0:T(8,128)}, f32[8,128]{1,0:T(8,128)}) custom-call(bf16[1,256]{1,0:T(2,128)(2,1)} %draws_ref.1, bf16[2048,512]{1,0:T(8,128)(2,1)} %bitcast.5, bf16[512,512]{1,0:T(8,128)(2,1)} %bitcast.6, bf16[512,128]{1,0:T(8,128)(2,1)} %bitcast.8), custom_call_target="tpu_custom_call" | custom-call | tf_op jit(solution)/shard_map/step/pallas_call | solution.py:476
  105.4 1.2 %slice.3 = f32[1,1]{1,0:T(1,128)} slice(f32[8,128]{1,0:T(8,128)} %get-tuple-element.5), slice={[0:1], [0:1]} | slice | bytes 8 | tf_op jit(solution)/shard_map/slice | solution.py:514
  106.6 1.7 %copy.7 = f32[1,512,128]{2,1,0:T(8,128)} copy(f32[1,512,128]{2,1,0:T(8,128)} %bitcast.7) | data formatting | bytes 524288

commit v4 on v3

--- a/solution.py
+++ b/solution.py
@@ -106,11 +106,11 @@
 def step_kernel(
     draws_ref, chol_hbm, rot_hbm, walker_ref, prop_out, energy_out,
     chol_buf, draw_row, gathered, spreads, acc, part, recv, red, oper, rall, prop, corr, duals,
-    pieces, collected, answer,
+    pieces, collected,
     chol_sem, rot_sem, draw_send, draw_recv, part_send, part_recv,
     row_send, row_recv, x_send, x_recv, sib_send, sib_recv,
     z_send, z_recv, y_send, y_recv, prop_send, prop_recv,
-    piece_send, piece_recv, final_send, final_recv,
+    piece_send, piece_recv,
 ):
     chol, walk = here()
     z = walk // 4
@@ -145,16 +145,30 @@
         greet(to((chol + i) % 8, walk))
         return carry
 
+    x_from = (z % 8) // 2
+
+    def greet_pieces(i, carry):
+        other_chol = x_from * 2 + i // 32
+        other_walk = (i % 32) * 2 + core
+        same = jnp.logical_and(other_chol == chol, other_walk == walk)
+
+        @pl.when(jnp.logical_not(same))
+        def _():
+            greet(to(other_chol, other_walk))
+
+        return carry
+
     lax.fori_loop(1, 64, greet_walk, 0)
     lax.fori_loop(1, 8, greet_chol, 0)
     lax.fori_loop(0, 32, greet_plane, 0)
+    lax.fori_loop(0, 64, greet_pieces, 0)
     load_chol = pltpu.make_async_copy(chol_hbm, chol_buf, chol_sem)
     load_chol.start()
     load_rot = pltpu.make_async_copy(rot_hbm, rall.at[x, core], rot_sem)
     load_rot.start()
     draw_row[...] = draws_ref[...].astype(jnp.float32)
     slot = (z % 8) * 8 + (z // 8) * 4 + walk % 4
-    pl.semaphore_wait(barrier, 63 + 7 + 32)
+    pl.semaphore_wait(barrier, 63 + 7 + 32 + jnp.where(x_from == x, 63, 64))
 
     own_draw = pltpu.make_async_copy(draw_row, gathered.at[slot], draw_recv)
     own_draw.start()
@@ -270,13 +284,13 @@
         invert(corr)
         duals[y, z // 8] = jnp.dot(
             prop[...], corr[...], precision=HIGHEST, preferred_element_type=jnp.float32
-        ).astype(jnp.bfloat16)
-
-    def hop(which, kind):
-        block = duals.at[y, which]
+        ).astype(jnp.bfloat16).reshape(2, 256, OCC)
+
+    def hop(which, half, kind):
+        block = duals.at[y, which, half]
         return remote(
-            block, block, z_send.at[which, kind], z_recv.at[which],
-            at((z + (4, 12, 1, 15)[kind]) % 16, y),
+            block, block, z_send.at[which, half, kind], z_recv.at[which, half],
+            at((z + (6, 10, 3, 13, 2, 14, 1, 15)[kind]) % 16, y),
         )
 
     def away(which):
@@ -288,58 +302,70 @@
             found = jnp.logical_or(found, value == option)
         return found
 
-    def hops(which):
+    def relays(which):
         d = away(which)
+        hub = any_of(d, (3, 13, 6, 10))
         return (
-            jnp.logical_or(d == 0, jnp.logical_and(d == 4, core == 0)),
-            jnp.logical_or(d == 0, jnp.logical_and(d == 12, core == 1)),
-            any_of(d, (0, 1, 4, 5, 8, 12)),
-            any_of(d, (0, 15, 4, 12, 11, 8)),
-        )
-
-    def y_copy(which, i):
-        block = duals.at[y, which]
+            (4, jnp.logical_and(d == 6, core == 0)),
+            (5, jnp.logical_and(d == 10, core == 1)),
+            (6, hub),
+            (7, hub),
+        )
+
+    def y_copy(which, half, i):
+        block = duals.at[y, which, half]
         return remote(
-            block, block, y_send.at[which, i - 1], y_recv.at[which, i - 1], at(z, (y + i) % 4)
+            block, block, y_send.at[which, half, i - 1], y_recv.at[which, half, i - 1],
+            at(z, (y + i) % 4),
         )
 
     step = 1 + 2 * core
 
-    def y_relay(which):
-        block = duals.at[(y + 4 - step) % 4, which]
+    def y_relay(which, half):
+        block = duals.at[(y + 4 - step) % 4, which, half]
         return remote(
-            block, block, y_send.at[which, 1], y_recv.at[which, 1], at(z, (y + step) % 4)
-        )
-
-    def settle(which):
-        block = duals.at[y, which]
+            block, block, y_send.at[which, half, 1], y_recv.at[which, half, 1],
+            at(z, (y + step) % 4),
+        )
+
+    def settle(which, half):
+        block = duals.at[y, which, half]
 
         @pl.when(away(which) != 0)
         def _():
-            pltpu.make_async_copy(block, block, z_recv.at[which]).wait()
-
-        for kind, condition in enumerate(hops(which)):
+            pltpu.make_async_copy(block, block, z_recv.at[which, half]).wait()
+
+        for kind, condition in relays(which):
 
             @pl.when(condition)
             def _():
-                hop(which, kind).start()
-
-        y_copy(which, 1).start()
-        y_copy(which, 3).start()
-
-    def pass_on(which):
-        block = duals.at[(y + 4 - step) % 4, which]
-        pltpu.make_async_copy(block, block, y_recv.at[which, step - 1]).wait()
-        y_relay(which).start()
-
-    d = away(0)
-    first = jnp.where(jnp.logical_or(d <= 4, d >= 12), 0, 1)
-    settle(first)
-    settle(1 - first)
-    pass_on(first)
+                hop(which, half, kind).start()
+
+        y_copy(which, half, 1).start()
+        y_copy(which, half, 3).start()
+
+    def pass_on(which, half):
+        block = duals.at[(y + 4 - step) % 4, which, half]
+        pltpu.make_async_copy(block, block, y_recv.at[which, half, step - 1]).wait()
+        y_relay(which, half).start()
+
+    @pl.when(computes)
+    def _():
+        for kinds in ((0, 1), (2, 3), (6, 7)):
+            for half in (0, 1):
+                for kind in kinds:
+                    hop(z // 8, half, kind).start()
+
+    first = jnp.where(any_of(away(0), (0, 1, 15, 3, 13, 6, 10)), 0, 1)
+    for which in (first, 1 - first):
+        for half in (0, 1):
+            settle(which, half)
+    pass_on(first, 0)
+    pass_on(first, 1)
     x_copy(2).wait_recv()
     sib_copy(2).start()
-    pass_on(1 - first)
+    pass_on(1 - first, 0)
+    pass_on(1 - first, 1)
 
     def prop_copy(i):
         return remote(prop, prop_out, prop_send.at[i - 1], prop_recv, to((chol + i) % 8, walk))
@@ -354,7 +380,9 @@
         sib_copy(i).wait_recv()
 
     def pair_energy(yy):
-        block = jnp.concatenate([duals[yy, 0], duals[yy, 1]], axis=1)
+        block = jnp.concatenate(
+            [duals[yy, which].reshape(ORB, OCC) for which in (0, 1)], axis=1
+        )
 
         def vectors(i, sums):
             rows = rall[i].reshape(1024, ORB)
@@ -370,28 +398,28 @@
 
         zero = jnp.zeros((8, 128), jnp.float32)
         sums = lax.fori_loop(0, 4, vectors, (zero, zero))
-        pieces[yy, 0] = sums[0]
-        pieces[yy, 1] = sums[1]
-
-    def piece_copy(yy, which):
-        return remote(
-            pieces.at[yy, which], collected.at[z * 4 + y], piece_send.at[yy, which], piece_recv,
-            at(which * 8 + 2 * x + yy // 2, yy),
-        )
-
-    def is_me(yy, which):
-        return jnp.logical_and(yy == y, z == which * 8 + 2 * x + yy // 2)
+        for which in (0, 1):
+            pieces[yy, which] = jnp.sum(sums[which], axis=0, keepdims=True)
 
     def send_piece(yy, which):
-        @pl.when(jnp.logical_not(is_me(yy, which)))
-        def _():
-            piece_copy(yy, which).start()
-
-        @pl.when(is_me(yy, which))
-        def _():
-            pltpu.make_async_copy(
-                pieces.at[yy, which], collected.at[z * 4 + y], piece_recv
-            ).start()
+        target = (which * 8 + 2 * x + yy // 2) * 4 + (yy % 2) * 2 + core
+        piece = pieces.at[yy, which]
+        place = collected.at[z * 4 + y]
+
+        def send_to(peer, carry):
+            same = jnp.logical_and(target == walk, peer == chol)
+
+            @pl.when(jnp.logical_not(same))
+            def _():
+                remote(piece, place, piece_send, piece_recv, to(peer, target)).start()
+
+            @pl.when(same)
+            def _():
+                pltpu.make_async_copy(piece, place, piece_recv).start()
+
+            return carry
+
+        lax.fori_loop(0, 8, send_to, 0)
 
     def each_pair(n, carry):
         i = jnp.where(n == 2, 3, jnp.where(n == 3, 2, n))
@@ -400,8 +428,9 @@
         @pl.when(jnp.logical_and(n > 0, i != step))
         def _():
             for which in (0, 1):
-                block = duals.at[yy, which]
-                pltpu.make_async_copy(block, block, y_recv.at[which, i - 1]).wait()
+                for half in (0, 1):
+                    block = duals.at[yy, which, half]
+                    pltpu.make_async_copy(block, block, y_recv.at[which, half, i - 1]).wait()
 
         pair_energy(yy)
         for which in (0, 1):
@@ -409,21 +438,6 @@
         return carry
 
     lax.fori_loop(0, 4, each_pair, 0)
-
-    def final_copy(i):
-        return remote(
-            answer.at[0], answer.at[1], final_send.at[i - 1], final_recv, to((chol + i) % 8, walk)
-        )
-
-    @pl.when(computes)
-    def _():
-        pltpu.make_async_copy(collected, collected, piece_recv).wait()
-        lanes = jnp.sum(jnp.sum(collected[...], axis=0), axis=0, keepdims=True)
-        value = -0.5 * jnp.sum(lanes, axis=1, keepdims=True)
-        answer[0] = jnp.broadcast_to(value, (8, 128))
-        for i in range(1, 8):
-            final_copy(i).start()
-        pltpu.make_async_copy(answer.at[0], answer.at[1], final_recv).start()
 
     def drain_rows(j, carry):
         @pl.when(row_target(j) != walk)
@@ -443,31 +457,46 @@
     for i in range(4):
         sib_copy(i).wait_send()
     for which in (0, 1):
-        for kind, condition in enumerate(hops(which)):
-
-            @pl.when(condition)
-            def _():
-                hop(which, kind).wait_send()
-
-        y_copy(which, 1).wait_send()
-        y_copy(which, 3).wait_send()
-        y_relay(which).wait_send()
-        for yy in range(4):
-
-            @pl.when(jnp.logical_not(is_me(yy, which)))
-            def _():
-                piece_copy(yy, which).wait_send()
-
-    pltpu.make_async_copy(prop_out, prop_out, prop_recv).wait()
+        for half in (0, 1):
+            for kind, condition in relays(which):
+
+                @pl.when(condition)
+                def _():
+                    hop(which, half, kind).wait_send()
+
+            y_copy(which, half, 1).wait_send()
+            y_copy(which, half, 3).wait_send()
+            y_relay(which, half).wait_send()
 
     @pl.when(computes)
     def _():
+        for half in (0, 1):
+            for kind in (0, 1, 2, 3, 6, 7):
+                hop(z // 8, half, kind).wait_send()
         for i in range(1, 8):
             prop_copy(i).wait_send()
-            final_copy(i).wait_send()
-
-    pltpu.make_async_copy(answer.at[1], answer.at[1], final_recv).wait()
-    energy_out[...] = answer[1]
+
+    def pieces_sent(count):
+        gone = collected.at[pl.ds(0, count)]
+        pltpu.make_async_copy(gone, gone, piece_send).wait()
+
+    @pl.when(x_from == x)
+    def _():
+        pieces_sent(63)
+
+    @pl.when(x_from != x)
+    def _():
+        pieces_sent(64)
+
+    pltpu.make_async_copy(prop_out, prop_out, prop_recv).wait()
+    pltpu.make_async_copy(collected, collected, piece_recv).wait()
+    lanes = jnp.sum(collected[...].reshape(64, OCC), axis=0, keepdims=True)
+    energy_out[...] = jnp.broadcast_to(-0.5 * jnp.sum(lanes, axis=1, keepdims=True), (8, 128))
+
+
+def finish_kernel(prop_ref, energy_ref, prop_out, energy_out):
+    prop_out[...] = prop_ref[...]
+    energy_out[0] = energy_ref[0, 0]
 
 
 def per_device(field_draws, chol_vectors, rotated_vectors, walkers):
@@ -494,14 +523,13 @@
             VMEM((4, 2, 512, ORB), jnp.bfloat16),
             VMEM((ORB, OCC), jnp.float32),
             VMEM((OCC, OCC), jnp.float32),
-            VMEM((4, 2, ORB, OCC), jnp.bfloat16),
-            VMEM((4, 2, 8, 128), jnp.float32),
-            VMEM((64, 8, 128), jnp.float32),
-            VMEM((2, 8, 128), jnp.float32),
+            VMEM((4, 2, 2, 256, OCC), jnp.bfloat16),
+            VMEM((4, 2, 1, 128), jnp.float32),
+            VMEM((64, 1, 128), jnp.float32),
             DMA, DMA, DMA, DMA, DMA((2, 7)), DMA((2, 7)),
             DMA((8,)), DMA, DMA((3,)), DMA((3,)), DMA((4,)), DMA((4,)),
-            DMA((2, 4)), DMA((2,)), DMA((2, 3)), DMA((2, 3)), DMA((7,)), DMA,
-            DMA((4, 2)), DMA, DMA((7,)), DMA,
+            DMA((2, 2, 8)), DMA((2, 2)), DMA((2, 2, 3)), DMA((2, 2, 3)), DMA((7,)), DMA,
+            DMA, DMA,
         ],
         compiler_params=pltpu.CompilerParams(collective_id=0, has_side_effects=True),
         name="step",
@@ -511,7 +539,17 @@
         rotated_vectors.reshape(512, ORB),
         walkers.reshape(ORB, OCC),
     )
-    return (propagated.reshape(1, ORB, OCC), exchange[0, 0:1])
+    propagated, exchange = pl.pallas_call(
+        finish_kernel,
+        out_shape=(
+            jax.ShapeDtypeStruct((ORB, OCC), jnp.float32),
+            jax.ShapeDtypeStruct((1,), jnp.float32),
+        ),
+        in_specs=[vmem, vmem],
+        out_specs=(vmem, pl.BlockSpec(memory_space=pltpu.SMEM)),
+        name="finish",
+    )(propagated, exchange)
+    return (propagated.reshape(1, ORB, OCC), exchange)
 
 
 def solution(mesh):

time: 108 us -> 104 us (0.963)
  the two profiles are of different devices: /device:TPU:36 before, /device:TPU:34 now
where the time goes in v4:
time: 104 us
  Pallas kernels  104 us (100%)
    pallas_call x1, Pallas kernels, per_device(): pl.pallas_call(step_kernel, out_shape=(jax.ShapeDtypeStruct((ORB, OCC), j...  102 us

profile of v4, /device:TPU:34, one launch (start us, length us, event | category | flops | bytes accessed | tf_op | source)
XLA Modules:
  0.0 104.2 jit_solution(9742409170338186056)
XLA Ops:
  0.6 101.9 %step.1 = (f32[512,128]{1,0:T(8,128)}, f32[8,128]{1,0:T(8,128)}) custom-call(bf16[1,256]{1,0:T(2,128)(2,1)} %draws_ref.1, bf16[2048,512]{1,0:T(8,128)(2,1)} %bitcast.4, bf16[512,512]{1,0:T(8,128)(2,1)} %bitcast.5, bf16[512,128]{1,0:T(8,128)(2,1)} %bitcast.6), custom_call_target="tpu_custom_call" | custom-call | tf_op jit(solution)/shard_map/step/pallas_call | solution.py:505
  102.6 1.7 %finish.1 = (f32[512,128]{1,0:T(8,128)}, f32[1]{0:T(128)}) custom-call(f32[512,128]{1,0:T(8,128)} %get-tuple-element.6.prop_ref, f32[8,128]{1,0:T(8,128)} %get-tuple-element.7.energy_ref), custom_call_target="tpu_custom_call" | custom-call | tf_op jit(solution)/shard_map/finish/pallas_call | solution.py:542
